TPU v7x, 256 devices: a whole 4x4x8 slice. The times are simulated.
256 devices in a mesh: prompt: 4 (over x), vocab: 64 (over z, y, core).
Axes of the slice: x: 4, y: 4, z: 8, core: 2. Of those that a mesh axis runs over, the one named last changes fastest.
Arguments:
- hidden: bfloat16 [512, 8192], P('prompt')
- head: bfloat16 [8192, 65536], P('prompt', 'vocab')
- gain: float32 [8192], replicated, may hold values from 0.25 to 1.75
- refusal_ids: int32 [512, 16], P('prompt'), may hold values from 0 to 65535, as said below
- refusal_count: int32 [512], P('prompt'), may hold values from 1 to 16
- loss_scale: float32 [512], P('prompt'), may hold values from 8 to 32
Outputs:
- grad_hidden: float32 [512, 8192], P('prompt', 'vocab')
- log_refusal: float32 [512], P('prompt')
Inputs may be any that keep to these rules, and one draw needn't show every extreme that they name: `refusal_ids`: the first refusal_count entries of a prompt's list are distinct ids below 65536; later entries are ignored.
All inputs are finite; a program needn't handle non-finite values.
Results may differ from a plain program's by a relative error of at most 0.0027.
The roundings to bfloat16 on the way count: a program that leaves them out, or rounds other values in their place, can miss the bound.
Values may be sent and summed in bfloat16 or wider, within the bound.
A program may use at most 128 MiB of HBM per device.

v0:
```python
import jax
import jax.numpy as jnp
from jax import lax
from jax.sharding import PartitionSpec as P

epsilon = 1e-05
lowest = -1e30


def shards(hidden, head, gain, refusal_ids, refusal_count, loss_scale):
    row_count, model_width = hidden.shape
    vocab_local = head.shape[1]
    list_length = refusal_ids.shape[1]
    hidden_f = hidden.astype(jnp.float32)
    inverse_rms = lax.rsqrt(jnp.mean(hidden_f * hidden_f, axis=1, keepdims=True) + epsilon)
    normed = (hidden_f * inverse_rms * gain).astype(jnp.bfloat16)
    logits = jnp.dot(
        normed,
        lax.all_gather(head, "prompt", axis=0, tiled=True),
        preferred_element_type=jnp.float32,
    )
    vocab_start = lax.axis_index("vocab") * vocab_local
    shifted_ids = refusal_ids - vocab_start
    in_list = jnp.arange(list_length)[None, :] < refusal_count[:, None]
    is_local = in_list & (shifted_ids >= 0) & (shifted_ids < vocab_local)
    safe_ids = jnp.clip(shifted_ids, 0, vocab_local - 1)
    picked = jnp.take_along_axis(logits, safe_ids, axis=1)
    peak_all = jnp.max(logits, axis=1)
    peak_ref = jnp.max(jnp.where(is_local, picked, lowest), axis=1)
    peak_all, peak_ref = lax.pmax((peak_all, peak_ref), "vocab")
    sum_all = jnp.sum(jnp.exp(logits - peak_all[:, None]), axis=1)
    sum_ref = jnp.sum(jnp.exp(jnp.where(is_local, picked - peak_ref[:, None], lowest)), axis=1)
    sum_all, sum_ref = lax.psum((sum_all, sum_ref), "vocab")
    lse_all = peak_all + jnp.log(sum_all)
    lse_ref = peak_ref + jnp.log(sum_ref)
    log_refusal = lse_ref - lse_all
    member = jnp.any(
        (safe_ids[:, :, None] == jnp.arange(vocab_local)[None, None, :]) & is_local[:, :, None],
        axis=1,
    )
    grad_logits = loss_scale[:, None] * (
        jnp.exp(jnp.where(member, logits - lse_ref[:, None], lowest))
        - jnp.exp(logits - lse_all[:, None])
    )
    grad_b = grad_logits.astype(jnp.bfloat16)
    slice_width = model_width // lax.axis_size("vocab")
    col_start = lax.axis_index("vocab") * slice_width
    grad_full = lax.dot_general(
        grad_b,
        lax.all_gather(head, "prompt", axis=0, tiled=True),
        (((1,), (1,)), ((), ())),
        preferred_element_type=jnp.float32,
    )
    grad_cols = lax.psum_scatter(grad_full, "vocab", scatter_dimension=1, tiled=True)
    normed_cols = lax.dynamic_slice_in_dim(normed, col_start, slice_width, 1).astype(jnp.float32)
    row_term = lax.psum(jnp.sum(grad_cols * normed_cols, axis=1), "vocab")
    hidden_cols = lax.dynamic_slice_in_dim(hidden_f, col_start, slice_width, 1)
    gain_cols = lax.dynamic_slice_in_dim(gain, col_start, slice_width, 0)
    grad_hidden = (
        inverse_rms * gain_cols * grad_cols
        - hidden_cols * (inverse_rms * inverse_rms / model_width) * row_term[:, None]
    )
    return (grad_hidden, log_refusal)


def solution(mesh):
    return jax.shard_map(
        shards,
        mesh=mesh,
        in_specs=(
            P("prompt", None),
            P("prompt", "vocab"),
            P(),
            P("prompt", None),
            P("prompt"),
            P("prompt"),
        ),
        out_specs=(P("prompt", "vocab"), P("prompt")),
        check_vma=False,
    )
```

profile of v0, /device:TPU:4, one launch (start us, length us, event | category | flops | bytes accessed | tf_op | source)
XLA Modules:
  0.0 738.3 jit_solution(6245504685200072266)
XLA Ops:
  7.2 0.0 copy-start.2
  7.2 0.0 copy-start
  7.2 0.0 copy-start.1
  7.2 0.0 all-gather.2.cloned.1.call-start
  7.2 0.7 all-gather.2.cloned.1.call-update
  7.9 0.0 reduce-scatter.2.cloned.1.call-start
  8.0 0.0 copy-done.2
  8.0 0.1 copy.11
  8.1 0.1 reshape.39
  8.2 0.6 copy-done
  8.8 0.5 multiply_reduce_fusion
  9.3 0.0 copy-done.1
  9.3 1.9 multiply_convert_fusion
  11.2 157.9 %all-gather.2.cloned.1.call-done = bf16[8192,1024]{1,0:T(8,128)(2,1)} async-done(((bf16[2048,1024]{1,0:T(8,128)(2,1)}), bf16[8192,1024]{1,0:T(8,128)(2,1)}) %all-gather.2.cloned.1.call-update) | async-done | bytes 16777232 | tf_op jit(solution)/shard_map/all_gather | solution.py:19
  169.1 8.8 %fusion.12 = (f32[128]{0:T(128)S(1)}, f32[128,1024]{1,0:T(8,128)S(1)}) fusion(bf16[128,8192]{1,0:T(8,128)(2,1)} %multiply_convert_fusion, bf16[8192,1024]{1,0:T(8,128)(2,1)} %all-gather.2.cloned.1.call-done), kind=kOutput, calls=%fused_computation.30 | convolution fusion | flops 2147614720 | bytes 19399168 | tf_op jit(solution)/shard_map/dot_general | solution.py:17
  178.0 0.0 copy-start.4
  178.0 0.0 copy-start.3
  178.0 16.6 %gather_fusion = f32[2048]{0:T(1024)S(1)} fusion(f32[128,1024]{1,0:T(8,128)S(1)} %get-tuple-element.16, s32[2048]{0:T(1024)S(1)} %reshape.39), kind=kCustom, calls=%fused_computation | custom fusion | bytes 32768 | tf_op jit(solution)/shard_map/jit(take_along_axis)/gather | solution.py:27
  194.6 0.1 reshape.42
  194.7 0.0 copy-done.4
  194.7 0.2 select_reduce_fusion
  194.9 2.4 fusion.1
  197.3 129.0 %all-reduce.1 = (f32[128]{0:T(128)S(1)}, f32[128]{0:T(128)S(1)}) all-reduce(f32[128]{0:T(128)S(1)} %get-tuple-element.15, f32[128]{0:T(128)S(1)} %get-tuple-element.9), channel_id=1, replica_groups=mesh['prompt'=4,'vocab'=64] {'vocab'}, use_global_device_ids=true, to_apply=%region_7.8 | all-reduce | flops 256 | bytes 2048 | tf_op jit(solution)/shard_map/pmax | solution.py:30
  326.3 0.2 exponential_reduce_fusion.1
  326.5 0.2 exponential_reduce_fusion
  326.7 124.1 %all-reduce = (f32[128]{0:T(128)S(1)}, f32[128]{0:T(128)S(1)}) all-reduce(f32[128]{0:T(128)S(1)} %exponential_reduce_fusion, f32[128]{0:T(128)S(1)} %exponential_reduce_fusion.1), channel_id=1, replica_groups=mesh['prompt'=4,'vocab'=64] {'vocab'}, use_global_device_ids=true, to_apply=%region_9.10 | all-reduce | flops 256 | bytes 2048 | tf_op jit(solution)/shard_map/psum | solution.py:33
  450.8 0.5 fusion.10
  451.3 0.0 copy-done.3
  451.3 13.4 %fusion.2 = f32[128,8192]{1,0:T(8,128)} fusion(bf16[8192,1024]{1,0:T(8,128)(2,1)} %all-gather.2.cloned.1.call-done, f32[128,1024]{1,0:T(8,128)S(1)} %get-tuple-element.16, pred[128,1024]{1,0:T(8,128)(4,1)S(1)} %fusion.1, f32[128]{0:T(128)S(1)} %get-tuple-element.8, f32[128]{0:T(128)S(1)} %get-tuple-element.7, f32[128]{0:T(128)S(1)} %copy-done.3), kind=kOutput, calls=%fused_computation.8 | convolution fusion | flops 2148270080 | bytes 21628416 | tf_op jit(solution)/shard_map/dot_general | solution.py:48
  464.8 0.0 reduce-scatter.2.cloned.1.call-update
  464.8 2.3 convert_element_type.12
  467.1 0.1 dynamic_slice.9
  467.2 137.6 %reduce-scatter.2.cloned.1.call-done = f32[128,128]{1,0:T(8,128)} async-done(((f32[128,8192]{1,0:T(8,128)}), f32[128,128]{1,0:T(8,128)}) %reduce-scatter.2.cloned.1.call-update) | async-done | bytes 65552 | tf_op jit(solution)/shard_map/reduce_scatter | solution.py:54
  604.8 0.9 multiply_reduce_fusion.1
  605.8 124.1 %psum.23 = f32[128]{0:T(128)S(1)} all-reduce(f32[128]{0:T(128)S(1)} %multiply_reduce_fusion.1), channel_id=1, replica_groups=mesh['prompt'=4,'vocab'=64] {'vocab'}, use_global_device_ids=true, to_apply=%region_12.13 | all-reduce | flops 128 | bytes 1024 | tf_op jit(solution)/shard_map/psum | solution.py:56
  729.8 1.6 multiply_subtract_fusion
  (2 shorter events, 0.0 us)
Async XLA Ops:
  7.2 0.8 copy-start.2
  7.2 1.6 copy-start
  7.2 2.1 copy-start.1
  7.2 161.9 %all-gather.2.cloned.1.call-start = ((), (), s32[]{:S(2)}) async-start(), calls=%async_computation.1 | async-start | bytes 20971520 | tf_op jit(solution)/shard_map/all_gather | solution.py:19
  7.9 596.9 %reduce-scatter.2.cloned.1.call-start = ((), (), s32[]{:S(2)}) async-start(), calls=%async_computation.2 | async-start | bytes 4259840 | tf_op jit(solution)/shard_map/reduce_scatter | solution.py:54
  178.0 16.8 %copy-start.4 = (s32[128]{0:T(128)S(1)}, s32[128]{0:T(128)}, u32[]{:S(2)}) copy-start(s32[128]{0:T(128)} %param.10) | copy-start | bytes 1540
  178.0 273.3 %copy-start.3 = (f32[128]{0:T(128)S(1)}, f32[128]{0:T(128)}, u32[]{:S(2)}) copy-start(f32[128]{0:T(128)} %param.11) | copy-start | bytes 1540
Sparse Core Ops, SparseCore 0:
  9.8 159.2 all-gather.1
  464.9 139.8 reduce-scatter.1
where the time goes:
time: 739 us; the launch traced here: 738 us
  blocking collectives  377 us (51%)
  waiting for transfers between devices  296 us (40%)
  matrix products  22.3 us (3%)
  local copies, waits for them, and re-layouts  17.6 us (2%)
  between operations  14.2 us (2%)
  other arithmetic  10.9 us (1%)
    all_gather x1, waiting for transfers between devices, shards(): lax.all_gather(head, 'prompt', axis=0, tiled=True)  158 us
    reduce_scatter x1, waiting for transfers between devices, shards(): lax.psum_scatter(grad_full, 'vocab', scatter_dimension=1, tiled=True)  138 us
    pmax x1, blocking collectives, shards(): peak_all, peak_ref = lax.pmax((peak_all, peak_ref), 'vocab')  129 us
    psum x1, blocking collectives, shards(): sum_all, sum_ref = lax.psum((sum_all, sum_ref), 'vocab')  124 us
    psum x1, blocking collectives, shards(): row_term = lax.psum(jnp.sum(grad_cols * normed_cols, axis=1), 'vocab')  124 us
    gather x3, local copies, waits for them, and re-layouts, shards(): picked = jnp.take_along_axis(logits, safe_ids, axis=1)  16.8 us
  transfers between devices with their start and end apart: 2, of which 2 were waited for; matrix products, arithmetic and copies ran while one was open for 1% of the time, Pallas kernels for 0%

commit v1 on v0

v1 whole, which is shorter than its diff:
```python
import functools

import jax
import jax.numpy as jnp
from jax import lax
from jax.experimental import pallas as pl
from jax.experimental.pallas import tpu as pltpu
from jax.sharding import PartitionSpec as P

epsilon = 1e-05
lowest = -1e30
f32 = jnp.float32
bf16 = jnp.bfloat16

NX, NY, NZ, NC = 4, 4, 8, 2
R = 128
DL = 2048
VL = 1024
T = 256
KT = DL // T
VT = VL // T


class Wires:
    def __init__(self, send, recv):
        self.send, self.recv, self.used, self.open = send, recv, 0, []

    def describe(self, src, dst, device, index):
        return pltpu.make_async_remote_copy(
            src_ref=src,
            dst_ref=dst,
            send_sem=self.send.at[index],
            recv_sem=self.recv.at[index],
            device_id=device,
            device_id_type=pl.DeviceIdType.MESH,
        )

    def start(self, src, dst, device):
        copy = self.describe(src, dst, device, self.used)
        self.used += 1
        copy.start()
        self.open.append(copy)
        return copy

    def close(self):
        for copy in self.open:
            copy.wait_send()


def kernel(
    hid_hbm, head_hbm, gain_ref, ids_ref, count_ref, loss_ref, grad_ref, log_ref,
    hid, head, inv_v, nsend, nrm, ptwo, pright, pleft, pown, hl, hr, inl, inr,
    mask, eall, eref, st1, st2, rs1, rs2, gt, csend, crecv, own32,
    ytwo, yright, yleft, yhl, yhr, yinl, yinr, fsend, frecv,
    load_sems, send_sems, recv_sems, fsend_sems, frecv_sems,
):
    p = lax.axis_index("prompt")
    v = lax.axis_index("vocab")
    c = v % NC
    y = (v // NC) % NY
    z = v // (NC * NY)

    def at(x_=p, y_=y, z_=z, c_=c):
        return (x_, (z_ * NY + y_) * NC + c_)

    def x_by(d):
        return at(x_=(p + d) % NX)

    def y_by(d):
        return at(y_=(y + d) % NY)

    def z_by(d):
        return at(z_=(z + d) % NZ)

    j_own = y * NC + c

    def plane_by(d):
        j = (j_own + d) % (NY * NC)
        return at(y_=j // NC, c_=j % NC), j

    sibling = at(c_=1 - c)

    load_hid = pltpu.make_async_copy(hid_hbm, hid, load_sems.at[0])
    load_head = pltpu.make_async_copy(head_hbm, head, load_sems.at[1])
    load_hid.start()
    load_head.start()

    barrier = pltpu.get_barrier_semaphore()

    def greet(device):
        pl.semaphore_signal(
            barrier, inc=1, device_id=device, device_id_type=pl.DeviceIdType.MESH
        )

    for d in range(1, NX):
        greet(x_by(d))
    for d in range(1, NY * NC):
        greet(plane_by(d)[0])
    for d in range(1, NZ):
        greet(z_by(d))
    source = z // 2
    foreign = source != p
    for d in range(1, NX):
        for zl in range(2):

            @pl.when(z != 2 * p + zl)
            def _():
                greet(at(x_=(p + d) % NX, z_=2 * p + zl))

    for zs in range(NZ):

        @pl.when(jnp.logical_and(foreign, jnp.logical_and(zs != z, zs // 2 != p)))
        def _():
            greet(at(x_=source, z_=zs))

    wires = Wires(send_sems, recv_sems)

    lane = lax.broadcasted_iota(jnp.int32, (R, 128), 1)
    sub = lax.broadcasted_iota(jnp.int32, (R, 128), 0)

    def columns_of(rows):
        return jnp.concatenate([rows, jnp.zeros((R - 8, 128), f32)], axis=0).T

    load_hid.wait()

    def square(j, acc):
        x = hid[:, pl.ds(pl.multiple_of(j * 1024, 1024), 1024)].astype(f32)
        x = x * x
        for i in range(8):
            acc = acc + x[:, i * 128 : (i + 1) * 128]
        return acc

    acc = lax.fori_loop(0, 8, square, jnp.zeros((R, 128), f32))
    inv = lax.rsqrt(jnp.sum(acc, axis=1, keepdims=True) / 8192.0 + epsilon)
    inv_v[...] = jnp.broadcast_to(inv, (R, 128))

    def normed(col):
        col = pl.multiple_of(col, T)
        x = hid[:, pl.ds(col, T)].astype(f32)
        return (x * inv * gain_ref[:, pl.ds(col, T)]).astype(bf16)

    for d in (2, 1, 3):
        q = (p + d) % NX
        for j in range(4):
            nsend[d - 1, j] = normed(q * DL + (c * 4 + j) * T)

    met = (NX - 1) + (NY * NC - 1) + (NZ - 1)
    pl.semaphore_wait(barrier, met + jnp.where(foreign, 2 * NX + 3, NX - 1))

    half = pl.ds(c * 4, 4)
    ncopy = {}
    for d in (2, 1, 3):
        slot = NX - d
        ncopy[slot] = wires.start(nsend.at[d - 1], nrm.at[slot, half], x_by(d))
    for k in range(KT):
        nrm[0, k] = normed(p * DL + k * T)
    share = {}
    for slot in (2, 3, 1):
        ncopy[slot].wait_recv()
        share[slot] = wires.start(nrm.at[slot, half], nrm.at[slot, half], sibling)
    other = pl.ds((1 - c) * 4, 4)
    share_sems = {slot: i for i, slot in enumerate((2, 3, 1), wires.used - 3)}

    def wait_share(slot):
        wires.describe(
            nrm.at[slot, other], nrm.at[slot, other], sibling, share_sems[slot]
        ).wait_recv()

    load_head.wait()

    def partial(s, t):
        lhs = jnp.concatenate([nrm[s, k] for k in range(KT)], axis=1)
        return jnp.dot(lhs, head[:, t * T : (t + 1) * T], preferred_element_type=f32)

    right, left = x_by(1), x_by(NX - 1)
    wait_share(2)
    ch_l, ch_r, cin_l, cin_r = {}, {}, {}, {}
    for t in (0, 2, 1, 3):
        ptwo[t] = partial(2, t)
        if t < 2:
            ch_l[t] = wires.start(ptwo.at[t], hl.at[t], right)
        else:
            ch_r[t - 2] = wires.start(ptwo.at[t], hr.at[t - 2], left)
    wait_share(1)
    for t in (2, 3):
        pright[t] = partial(1, t)
        cin_l[t] = wires.start(pright.at[t], inl.at[t], right)
    wait_share(3)
    for t in (0, 1):
        pleft[t] = partial(3, t)
        cin_r[t] = wires.start(pleft.at[t], inr.at[t], left)
    for t in (0, 1):
        pright[t] = partial(1, t)
        pleft[t + 2] = partial(3, t + 2)
    for t in (0, 1):
        ch_l[t].wait_recv()
        pright[t] = pright[t] + hl[t]
        cin_l[t] = wires.start(pright.at[t], inl.at[t], right)
        ch_r[t].wait_recv()
        pleft[t + 2] = pleft[t + 2] + hr[t]
        cin_r[t + 2] = wires.start(pleft.at[t + 2], inr.at[t + 2], left)
    for t in range(VT):
        pown[t] = partial(0, t)

    cl = jnp.where(
        sub == 0,
        jnp.broadcast_to(count_ref[...].astype(f32), (R, 128)),
        jnp.where(sub == 1, jnp.broadcast_to(loss_ref[...], (R, 128)), 0.0),
    ).T
    count_col, loss_col = cl[:, 0:1], cl[:, 1:2]
    wide = lax.broadcasted_iota(jnp.int32, (R, T), 1)
    for t in range(VT):
        hit = jnp.zeros((R, T), jnp.int32)
        for k in range(16):
            here = ids_ref[:, k : k + 1] - (v * VL + t * T)
            here = jnp.where(count_col > float(k), here, -1)
            hit = jnp.where(wide == here, 1, hit)
        mask[t] = hit

    m_all = jnp.full((R, T), -3e38, f32)
    m_ref = jnp.full((R, T), lowest, f32)
    for t in (2, 3, 0, 1):
        cin_l[t].wait_recv()
        cin_r[t].wait_recv()
        logit = pown[t] + inl[t] + inr[t]
        pown[t] = logit
        m_all = jnp.maximum(m_all, logit)
        m_ref = jnp.maximum(m_ref, jnp.where(mask[t] > 0, logit, lowest))
    m_all = jnp.max(m_all, axis=1, keepdims=True)
    m_ref = jnp.max(m_ref, axis=1, keepdims=True)
    s_all = jnp.zeros((R, T), f32)
    s_ref = jnp.zeros((R, T), f32)
    for t in range(VT):
        logit = pown[t]
        e = jnp.exp(logit - m_all)
        r = jnp.exp(jnp.where(mask[t] > 0, logit - m_ref, lowest))
        eall[t] = e
        eref[t] = r
        s_all = s_all + e
        s_ref = s_ref + r
    s_all = jnp.sum(s_all, axis=1, keepdims=True)
    s_ref = jnp.sum(s_ref, axis=1, keepdims=True)

    packed = jnp.where(lane == 0, m_all, jnp.zeros((R, 128), f32))
    packed = jnp.where(lane == 1, m_ref, packed)
    packed = jnp.where(lane == 8, s_all, packed)
    packed = jnp.where(lane == 9, s_ref, packed)
    packed = packed.T
    st1[j_own, 0] = packed[0:8]
    st1[j_own, 1] = packed[8:16]

    def spread_plane(buf):
        first = wires.used
        for d in range(1, NY * NC):
            wires.start(buf.at[j_own], buf.at[j_own], plane_by(d)[0])
        return first

    def await_plane(buf, first):
        for d in range(1, NY * NC):
            device, j = plane_by(NY * NC - d)
            wires.describe(buf.at[j], buf.at[j], device, first + d - 1).wait_recv()

    def spread_line(buf):
        first = wires.used
        for d in range(1, NZ):
            wires.start(buf.at[z], buf.at[z], z_by(d))
        return first

    def await_line(buf, first):
        for d in range(1, NZ):
            zz = (z + NZ - d) % NZ
            wires.describe(buf.at[zz], buf.at[zz], at(z_=zz), first + d - 1).wait_recv()

    def merged(buf, n):
        peak = buf[0, 0]
        for j in range(1, n):
            peak = jnp.maximum(peak, buf[j, 0])
        total = buf[0, 1] * jnp.exp(buf[0, 0] - peak)
        for j in range(1, n):
            total = total + buf[j, 1] * jnp.exp(buf[j, 0] - peak)
        return peak, total

    first = spread_plane(st1)
    await_plane(st1, first)
    peak, total = merged(st1, NY * NC)
    st2[z, 0] = peak
    st2[z, 1] = total
    first = spread_line(st2)
    await_line(st2, first)
    peak, total = merged(st2, NZ)
    row8 = lax.broadcasted_iota(jnp.int32, (8, 128), 0)
    lse = peak + jnp.log(jnp.where(row8 < 2, total, 1.0))
    log_ref[...] = lse[1:2] - lse[0:1]
    lse_cols = columns_of(lse)
    f_all = loss_col * jnp.exp(m_all - lse_cols[:, 0:1])
    f_ref = loss_col * jnp.exp(m_ref - lse_cols[:, 1:2])

    rt = jnp.zeros((R, T), f32)
    to_right, to_left = {}, {}
    def gather(t_r, t_l):
        to_right[t_r] = wires.start(gt.at[0, t_r], gt.at[3, t_r], right)
        to_left[t_l] = wires.start(gt.at[0, t_l], gt.at[1, t_l], left)

    for pair in ((0, 2), (1, 3)):
        for t in pair:
            g = (eref[t] * f_ref - eall[t] * f_all).astype(bf16)
            gt[0, t] = g
            rt = rt + g.astype(f32) * pown[t]
        gather(*pair)
    gather(2, 0)
    gather(3, 1)
    rt = jnp.sum(rt, axis=1, keepdims=True)
    rs1[j_own] = jnp.where(lane == 0, rt, jnp.zeros((R, 128), f32)).T[0:8]
    rt_first = spread_plane(rs1)

    def grad_tile(s, j, cc):
        yy = (y + j) % NY
        lhs = jnp.concatenate([gt[s, t] for t in range(VT)], axis=1)
        top = pl.multiple_of((yy * NC + cc) * 128, 128)
        low = pl.multiple_of(((NY + yy) * NC + cc) * 128, 128)
        rhs = jnp.concatenate([head[pl.ds(top, 128), :], head[pl.ds(low, 128), :]], axis=0)
        return lax.dot_general(
            lhs, rhs, (((1,), (1,)), ((), ())), preferred_element_type=f32
        )

    ccopy, yl2, yr2, yl, yr = {}, {}, {}, {}, {}
    up, down = y_by(1), y_by(NY - 1)

    def multiply(s):
        for j in (2, 1, 3, 0):
            csend[s, j] = grad_tile(s, j, 1 - c)
        ccopy[s] = wires.start(csend.at[s], crecv.at[s], sibling)
        for j in (2, 1, 3, 0):
            own32[s, j] = grad_tile(s, j, c)

    def y_first(s):
        ccopy[s].wait_recv()
        two = own32[s, 2] + crecv[s, 2]
        ytwo[s, 0] = two[:, :128].astype(bf16)
        ytwo[s, 1] = two[:, 128:].astype(bf16)
        yl2[s] = wires.start(ytwo.at[s, 0], yhl.at[s], up)
        yr2[s] = wires.start(ytwo.at[s, 1], yhr.at[s], down)
        one = own32[s, 1] + crecv[s, 1]
        own32[s, 1] = one
        yright[s, 1] = one[:, 128:].astype(bf16)
        yl[s, 1] = wires.start(yright.at[s, 1], yinl.at[s, 1], up)
        one = own32[s, 3] + crecv[s, 3]
        own32[s, 3] = one
        yleft[s, 0] = one[:, :128].astype(bf16)
        yr[s, 0] = wires.start(yleft.at[s, 0], yinr.at[s, 0], down)

    def y_second(s):
        yl2[s].wait_recv()
        yright[s, 0] = (own32[s, 1, :, :128] + yhl[s].astype(f32)).astype(bf16)
        yl[s, 0] = wires.start(yright.at[s, 0], yinl.at[s, 0], up)
        yr2[s].wait_recv()
        yleft[s, 1] = (own32[s, 3, :, 128:] + yhr[s].astype(f32)).astype(bf16)
        yr[s, 1] = wires.start(yleft.at[s, 1], yinr.at[s, 1], down)

    def place(s, zl):
        return pltpu.make_async_remote_copy(
            src_ref=fsend.at[s, zl],
            dst_ref=frecv.at[z],
            send_sem=fsend_sems.at[s * 2 + zl],
            recv_sem=frecv_sems.at[z],
            device_id=at(x_=(p + s) % NX, z_=2 * p + zl),
            device_id_type=pl.DeviceIdType.MESH,
        )

    def y_third(s):
        for zl in (1, 0):
            yl[s, zl].wait_recv()
            yr[s, zl].wait_recv()
            lanes = slice(zl * 128, zl * 128 + 128)
            out = own32[s, 0, :, lanes] + crecv[s, 0, :, lanes]
            out = out + yinl[s, zl].astype(f32) + yinr[s, zl].astype(f32)
            fsend[s, zl] = out
            if s:
                place(s, zl).start()
            else:

                @pl.when(z != 2 * p + zl)
                def _():
                    place(s, zl).start()

                @pl.when(z == 2 * p + zl)
                def _():
                    frecv[z] = fsend[s, zl]

    multiply(0)
    for t in (0, 1):
        to_right[t].wait_recv()
        wires.start(gt.at[3, t], gt.at[2, t], right)
        to_left[t + 2].wait_recv()
        wires.start(gt.at[1, t + 2], gt.at[2, t + 2], left)
    forward = wires.used - 4
    y_first(0)
    for t in (2, 3):
        to_right[t].wait_recv()
    multiply(3)
    y_second(0)
    for t in (0, 1):
        to_left[t].wait_recv()
    multiply(1)
    y_first(3)
    y_third(0)
    y_first(1)
    y_second(3)
    await_plane(rs1, rt_first)
    total = rs1[0]
    for j in range(1, NY * NC):
        total = total + rs1[j]
    rs2[z] = total
    rt_first = spread_line(rs2)
    for t in (0, 1):
        for i, tile, device in ((0, t, left), (1, t + 2, right)):
            wires.describe(
                gt.at[2, tile], gt.at[2, tile], device, forward + 2 * t + i
            ).wait_recv()
    multiply(2)
    y_second(1)
    y_third(3)
    y_first(2)
    y_third(1)
    y_second(2)
    await_line(rs2, rt_first)
    total = rs2[0]
    for j in range(1, NZ):
        total = total + rs2[j]
    rt_col = columns_of(total)[:, 0:1]
    y_third(2)

    own_cols = pl.ds(pl.multiple_of(v * 128, 128), 128)
    inv = inv_v[...]
    minus = hid[:, own_cols].astype(f32) * (inv * inv / 8192.0) * rt_col
    scale = inv * gain_ref[:, own_cols]
    for zs in range(NZ):

        @pl.when(jnp.logical_or(foreign, zs != z))
        def _():
            pltpu.make_async_remote_copy(
                src_ref=frecv.at[zs],
                dst_ref=frecv.at[zs],
                send_sem=fsend_sems.at[0],
                recv_sem=frecv_sems.at[zs],
                device_id=at(x_=source, z_=zs),
                device_id_type=pl.DeviceIdType.MESH,
            ).wait_recv()

    total = frecv[0]
    for zs in range(1, NZ):
        total = total + frecv[zs]
    grad_ref[...] = scale * total - minus

    wires.close()
    for s in range(NX):
        for zl in range(2):
            if s:
                place(s, zl).wait_send()
            else:

                @pl.when(z != 2 * p + zl)
                def _():
                    place(s, zl).wait_send()


def shards(hidden, head, gain, refusal_ids, refusal_count, loss_scale):
    V = pltpu.VMEM
    tile = (R, T)
    box = (R, 128)
    wires = 120
    grad, log_refusal = pl.pallas_call(
        kernel,
        out_shape=(
            jax.ShapeDtypeStruct((R, 128), f32),
            jax.ShapeDtypeStruct((1, R), f32),
        ),
        in_specs=[pl.BlockSpec(memory_space=pl.ANY)] * 2
        + [pl.BlockSpec(memory_space=pltpu.VMEM)] * 4,
        out_specs=(pl.BlockSpec(memory_space=pltpu.VMEM),) * 2,
        scratch_shapes=[
            V((R, NX * DL), bf16),
            V((DL, VL), bf16),
            V(box, f32),
            V((3, 4) + tile, bf16),
            V((NX, KT) + tile, bf16),
            V((VT,) + tile, f32),
            V((VT,) + tile, f32),
            V((VT,) + tile, f32),
            V((VT,) + tile, f32),
            V((2,) + tile, f32),
            V((2,) + tile, f32),
            V((VT,) + tile, f32),
            V((VT,) + tile, f32),
            V((VT,) + tile, jnp.int32),
            V((VT,) + tile, f32),
            V((VT,) + tile, f32),
            V((NY * NC, 2, 8, 128), f32),
            V((NZ, 2, 8, 128), f32),
            V((NY * NC, 8, 128), f32),
            V((NZ, 8, 128), f32),
            V((NX, VT) + tile, bf16),
            V((NX, NY) + tile, f32),
            V((NX, NY) + tile, f32),
            V((NX, NY) + tile, f32),
            V((NX, 2) + box, bf16),
            V((NX, 2) + box, bf16),
            V((NX, 2) + box, bf16),
            V((NX,) + box, bf16),
            V((NX,) + box, bf16),
            V((NX, 2) + box, bf16),
            V((NX, 2) + box, bf16),
            V((NX, 2) + box, f32),
            V((NZ,) + box, f32),
            pltpu.SemaphoreType.DMA((2,)),
            pltpu.SemaphoreType.DMA((wires,)),
            pltpu.SemaphoreType.DMA((wires,)),
            pltpu.SemaphoreType.DMA((NX * 2,)),
            pltpu.SemaphoreType.DMA((NZ,)),
        ],
        compiler_params=pltpu.CompilerParams(
            collective_id=0, has_side_effects=True, vmem_limit_bytes=48 << 20
        ),
        name="head_grad",
    )(
        hidden,
        head,
        gain.reshape(1, -1),
        refusal_ids,
        refusal_count.reshape(1, -1),
        loss_scale.reshape(1, -1),
    )
    return grad, log_refusal.reshape(-1)


def solution(mesh):
    return jax.shard_map(
        shards,
        mesh=mesh,
        in_specs=(
            P("prompt", None),
            P("prompt", "vocab"),
            P(),
            P("prompt", None),
            P("prompt"),
            P("prompt"),
        ),
        out_specs=(P("prompt", "vocab"), P("prompt")),
        check_vma=False,
    )
```

time: 739 us -> 112 us (0.15)
  blocking collectives: 377 us -> 0 us
  waiting for transfers between devices: 296 us -> 0 us
  Pallas kernels: 0 us -> 105 us
  matrix products: 22.3 us -> 0 us
  between operations: 14.2 us -> 0.65 us
  local copies, waits for them, and re-layouts: 17.6 us -> 5.59 us
  other arithmetic: 10.9 us -> 0 us
    psum x2 -> x0, blocking collectives: 248 us -> none  [the longest x1 124 us: shards(): sum_all, sum_ref = lax.psum((sum_all, sum_ref), 'vocab')]
    all_gather x1 -> x0, waiting for transfers between devices: 158 us -> none  [shards(): lax.all_gather(head, 'prompt', axis=0, tiled=True)]
    reduce_scatter x1 -> x0, waiting for transfers between devices: 138 us -> none  [shards(): lax.psum_scatter(grad_full, 'vocab', scatter_dimension=1, tiled=True)]
    pmax x1 -> x0, blocking collectives: 129 us -> none  [shards(): peak_all, peak_ref = lax.pmax((peak_all, peak_ref), 'vocab')]
    pallas_call x0 -> x1, Pallas kernels: none -> 105 us  [shards(): pl.pallas_call(kernel, out_shape=(jax.ShapeDtypeStruct((R, 128), f32), ja...]
    dot_general x2 -> x0, matrix products: 22.3 us -> none  [the longest x1 13.4 us: shards(): lax.dot_general(grad_b, lax.all_gather(head, 'prompt', axis=0, tiled=True...]
    gather x3 -> x0, local copies, waits for them, and re-layouts: 16.8 us -> none  [shards(): picked = jnp.take_along_axis(logits, safe_ids, axis=1)]
  transfers between devices with their start and end apart: 2 -> 0, of which waited for: 2 -> 0; matrix products, arithmetic and copies ran while one was open for 1% -> 0% of each run, Pallas kernels for 0% -> 0%
where the time goes in v1:
time: 112 us; the launch traced here: 111 us
  Pallas kernels  105 us (94%)
  local copies, waits for them, and re-layouts  5.59 us (5%)
    pallas_call x1, Pallas kernels, shards(): pl.pallas_call(kernel, out_shape=(jax.ShapeDtypeStruct((R, 128), f32), ja...  105 us
    unnamed x11, local copies, waits for them, and re-layouts  5.59 us

profile of v1, /device:TPU:4, one launch (start us, length us, event | category | flops | bytes accessed | tf_op | source)
XLA Modules:
  0.0 111.4 jit_solution(1822517981502089104)
XLA Ops:
  0.6 0.8 copy.8.ids_ref
  1.4 0.0 copy-start
  1.4 1.6 %copy-done = bf16[128,8192]{1,0:T(8,128)(2,1)S(1)} copy-done((bf16[128,8192]{1,0:T(8,128)(2,1)S(1)}, bf16[128,8192]{1,0:T(8,128)(2,1)}, u32[]{:S(2)}) %copy-start) | copy-done | bytes 2097176
  3.0 0.0 copy-start.1
  3.0 0.8 copy-done.1
  3.8 0.0 copy-start.2
  3.8 0.7 copy-done.2
  4.4 0.0 copy-start.3
  4.4 0.7 copy-done.3
  5.1 105.2 %head_grad.1 = (f32[128,128]{1,0:T(8,128)S(1)}, f32[1,128]{1,0:T(1,128)S(1)}) custom-call(bf16[128,8192]{1,0:T(8,128)(2,1)S(1)} %copy-done, bf16[2048,1024]{1,0:T(8,128)(2,1)} %head_hbm.1, f32[1,8192]{1,0:T(1,128)S(1)} %bitcast.4, s32[128,16]{1,0:T(8,128)S(1)} %copy.8.ids_ref, s32[1,128]{1,0:T(1,128)S(1)} %bitcast.5, f32[1,128]{1,0:T(1,128)S(1)} %bitcast.6), custom_call_target="tpu_custom_call" | custom-call | tf_op jit(solution)/shard_map/head_grad/pallas_call | solution.py:472
  110.2 0.6 copy.11
  110.9 0.5 copy.12
Async XLA Ops:
  1.4 1.6 %copy-start = (bf16[128,8192]{1,0:T(8,128)(2,1)S(1)}, bf16[128,8192]{1,0:T(8,128)(2,1)}, u32[]{:S(2)}) copy-start(bf16[128,8192]{1,0:T(8,128)(2,1)} %hid_hbm.1) | copy-start | bytes 6291460
  3.0 0.8 copy-start.1
  3.8 0.7 copy-start.2
  4.4 0.7 copy-start.3

commit v2 on v1

--- a/solution.py
+++ b/solution.py
@@ -48,10 +48,10 @@
 
 
 def kernel(
-    hid_hbm, head_hbm, gain_ref, ids_ref, count_ref, loss_ref, grad_ref, log_ref,
-    hid, head, inv_v, nsend, nrm, ptwo, pright, pleft, pown, hl, hr, inl, inr,
+    hid_hbm, head_hbm, gain_hbm, ids_hbm, count_hbm, loss_hbm, grad_ref, log_ref,
+    hid, head, gain_ref, ids_ref, count_ref, loss_ref, inv_v, nsend, nrm, ptwo, pright, pleft, pown, hl, hr, inl, inr,
     mask, eall, eref, st1, st2, rs1, rs2, gt, csend, crecv, own32,
-    ytwo, yright, yleft, yhl, yhr, yinl, yinr, fsend, frecv,
+    ytwo, yright, yleft, yhl, yhr, yinl, yinr, fsend, xrecv, frecv,
     load_sems, send_sems, recv_sems, fsend_sems, frecv_sems,
 ):
     p = lax.axis_index("prompt")
@@ -81,9 +81,14 @@
     sibling = at(c_=1 - c)
 
     load_hid = pltpu.make_async_copy(hid_hbm, hid, load_sems.at[0])
-    load_head = pltpu.make_async_copy(head_hbm, head, load_sems.at[1])
-    load_hid.start()
-    load_head.start()
+    load_gain = pltpu.make_async_copy(gain_hbm, gain_ref, load_sems.at[1])
+    load_head = pltpu.make_async_copy(head_hbm, head, load_sems.at[2])
+    load_ids = pltpu.make_async_copy(ids_hbm, ids_ref, load_sems.at[3])
+    load_count = pltpu.make_async_copy(count_hbm, count_ref, load_sems.at[4])
+    load_loss = pltpu.make_async_copy(loss_hbm, loss_ref, load_sems.at[5])
+    loads = (load_hid, load_gain, load_head, load_ids, load_count, load_loss)
+    for load in loads:
+        load.start()
 
     barrier = pltpu.get_barrier_semaphore()
 
@@ -98,21 +103,6 @@
         greet(plane_by(d)[0])
     for d in range(1, NZ):
         greet(z_by(d))
-    source = z // 2
-    foreign = source != p
-    for d in range(1, NX):
-        for zl in range(2):
-
-            @pl.when(z != 2 * p + zl)
-            def _():
-                greet(at(x_=(p + d) % NX, z_=2 * p + zl))
-
-    for zs in range(NZ):
-
-        @pl.when(jnp.logical_and(foreign, jnp.logical_and(zs != z, zs // 2 != p)))
-        def _():
-            greet(at(x_=source, z_=zs))
-
     wires = Wires(send_sems, recv_sems)
 
     lane = lax.broadcasted_iota(jnp.int32, (R, 128), 1)
@@ -133,46 +123,82 @@
     acc = lax.fori_loop(0, 8, square, jnp.zeros((R, 128), f32))
     inv = lax.rsqrt(jnp.sum(acc, axis=1, keepdims=True) / 8192.0 + epsilon)
     inv_v[...] = jnp.broadcast_to(inv, (R, 128))
+    load_gain.wait()
 
     def normed(col):
         col = pl.multiple_of(col, T)
         x = hid[:, pl.ds(col, T)].astype(f32)
         return (x * inv * gain_ref[:, pl.ds(col, T)]).astype(bf16)
 
+    k_own = c * NY + y
     for d in (2, 1, 3):
-        q = (p + d) % NX
-        for j in range(4):
-            nsend[d - 1, j] = normed(q * DL + (c * 4 + j) * T)
-
-    met = (NX - 1) + (NY * NC - 1) + (NZ - 1)
-    pl.semaphore_wait(barrier, met + jnp.where(foreign, 2 * NX + 3, NX - 1))
-
-    half = pl.ds(c * 4, 4)
-    ncopy = {}
+        nsend[d - 1] = normed((p + d) % NX * DL + k_own * T)
+
+    pl.semaphore_wait(barrier, (NX - 1) + (NY * NC - 1) + (NZ - 1))
+
+    up, down = y_by(1), y_by(NY - 1)
+    near = {d: c * NY + (y + d) % NY for d in range(NY)}
+    there = {d: (1 - c) * NY + (y + d) % NY for d in range(NY)}
+    first_half, second_half = pl.ds(0, R // 2), pl.ds(R // 2, R // 2)
+    come, go_up, go_down, far_up, far_down, shared = {}, {}, {}, {}, {}, {}
     for d in (2, 1, 3):
         slot = NX - d
-        ncopy[slot] = wires.start(nsend.at[d - 1], nrm.at[slot, half], x_by(d))
+        come[slot] = wires.start(nsend.at[d - 1], nrm.at[slot, k_own], x_by(d))
     for k in range(KT):
         nrm[0, k] = normed(p * DL + k * T)
-    share = {}
-    for slot in (2, 3, 1):
-        ncopy[slot].wait_recv()
-        share[slot] = wires.start(nrm.at[slot, half], nrm.at[slot, half], sibling)
-    other = pl.ds((1 - c) * 4, 4)
-    share_sems = {slot: i for i, slot in enumerate((2, 3, 1), wires.used - 3)}
+
+    def share(slot, d):
+        shared[slot, d] = wires.used
+        wires.start(nrm.at[slot, near[d]], nrm.at[slot, near[d]], sibling)
+
+    def arrived(slot, d, device, index, rows=None):
+        piece = nrm.at[slot, near[d]] if rows is None else nrm.at[slot, near[d], rows]
+        wires.describe(piece, piece, device, index).wait_recv()
+
+    def near_out(slot):
+        come[slot].wait_recv()
+        piece = nrm.at[slot, k_own]
+        go_up[slot] = wires.used
+        wires.start(piece, piece, up)
+        go_down[slot] = wires.used
+        wires.start(piece, piece, down)
+        share(slot, 0)
+
+    def far_out(slot):
+        arrived(slot, NY - 1, down, go_up[slot])
+        piece = nrm.at[slot, near[NY - 1], first_half]
+        far_up[slot] = wires.used
+        wires.start(piece, piece, up)
+        arrived(slot, 1, up, go_down[slot])
+        piece = nrm.at[slot, near[1], second_half]
+        far_down[slot] = wires.used
+        wires.start(piece, piece, down)
+        share(slot, NY - 1)
+        share(slot, 1)
+
+    def far_in(slot):
+        arrived(slot, 2, down, far_up[slot], first_half)
+        arrived(slot, 2, up, far_down[slot], second_half)
+        share(slot, 2)
 
     def wait_share(slot):
-        wires.describe(
-            nrm.at[slot, other], nrm.at[slot, other], sibling, share_sems[slot]
-        ).wait_recv()
-
-    load_head.wait()
+        for d in range(NY):
+            piece = nrm.at[slot, there[d]]
+            wires.describe(piece, piece, sibling, shared[slot, d]).wait_recv()
 
     def partial(s, t):
         lhs = jnp.concatenate([nrm[s, k] for k in range(KT)], axis=1)
         return jnp.dot(lhs, head[:, t * T : (t + 1) * T], preferred_element_type=f32)
 
     right, left = x_by(1), x_by(NX - 1)
+    near_out(2)
+    near_out(3)
+    near_out(1)
+    far_out(2)
+    far_in(2)
+    far_out(3)
+    far_out(1)
+    load_head.wait()
     wait_share(2)
     ch_l, ch_r, cin_l, cin_r = {}, {}, {}, {}
     for t in (0, 2, 1, 3):
@@ -181,6 +207,8 @@
             ch_l[t] = wires.start(ptwo.at[t], hl.at[t], right)
         else:
             ch_r[t - 2] = wires.start(ptwo.at[t], hr.at[t - 2], left)
+    far_in(3)
+    far_in(1)
     wait_share(1)
     for t in (2, 3):
         pright[t] = partial(1, t)
@@ -202,6 +230,10 @@
     for t in range(VT):
         pown[t] = partial(0, t)
 
+    load_ids.wait()
+    load_count.wait()
+    load_loss.wait()
+    ids = jnp.concatenate([ids_ref[...], jnp.zeros((R - 16, 128), jnp.int32)], axis=0).T
     cl = jnp.where(
         sub == 0,
         jnp.broadcast_to(count_ref[...].astype(f32), (R, 128)),
@@ -212,7 +244,7 @@
     for t in range(VT):
         hit = jnp.zeros((R, T), jnp.int32)
         for k in range(16):
-            here = ids_ref[:, k : k + 1] - (v * VL + t * T)
+            here = ids[:, k : k + 1] - (v * VL + t * T)
             here = jnp.where(count_col > float(k), here, -1)
             hit = jnp.where(wide == here, 1, hit)
         mask[t] = hit
@@ -303,9 +335,9 @@
 
     for pair in ((0, 2), (1, 3)):
         for t in pair:
-            g = (eref[t] * f_ref - eall[t] * f_all).astype(bf16)
-            gt[0, t] = g
-            rt = rt + g.astype(f32) * pown[t]
+            g = eref[t] * f_ref - eall[t] * f_all
+            gt[0, t] = g.T.astype(bf16)
+            rt = rt + g.astype(bf16).astype(f32) * pown[t]
         gather(*pair)
     gather(2, 0)
     gather(3, 1)
@@ -313,79 +345,84 @@
     rs1[j_own] = jnp.where(lane == 0, rt, jnp.zeros((R, 128), f32)).T[0:8]
     rt_first = spread_plane(rs1)
 
-    def grad_tile(s, j, cc):
-        yy = (y + j) % NY
-        lhs = jnp.concatenate([gt[s, t] for t in range(VT)], axis=1)
-        top = pl.multiple_of((yy * NC + cc) * 128, 128)
-        low = pl.multiple_of(((NY + yy) * NC + cc) * 128, 128)
-        rhs = jnp.concatenate([head[pl.ds(top, 128), :], head[pl.ds(low, 128), :]], axis=0)
-        return lax.dot_general(
-            lhs, rhs, (((1,), (1,)), ((), ())), preferred_element_type=f32
-        )
+    def grad_block(s, zl, cc):
+        rows = [
+            pl.multiple_of(((zl * NY + yy) * NC + cc) * 128, 128) for yy in range(NY)
+        ]
+        lhs = jnp.concatenate([head[pl.ds(row, 128), :] for row in rows], axis=0)
+        rhs = jnp.concatenate([gt[s, t] for t in range(VT)], axis=0)
+        out = jnp.dot(lhs, rhs, preferred_element_type=f32)
+        return out.reshape(NY, 128, R)
 
     ccopy, yl2, yr2, yl, yr = {}, {}, {}, {}, {}
-    up, down = y_by(1), y_by(NY - 1)
+    y1, y2, y3 = ((y + d) % NY for d in (1, 2, 3))
 
     def multiply(s):
-        for j in (2, 1, 3, 0):
-            csend[s, j] = grad_tile(s, j, 1 - c)
-        ccopy[s] = wires.start(csend.at[s], crecv.at[s], sibling)
-        for j in (2, 1, 3, 0):
-            own32[s, j] = grad_tile(s, j, c)
+        for zl in range(2):
+            csend[s, zl] = grad_block(s, zl, 1 - c)
+            ccopy[s, zl] = wires.start(csend.at[s, zl], crecv.at[s, zl], sibling)
+        for zl in range(2):
+            own32[s, zl] = grad_block(s, zl, c)
+
+    def pair_sum(s, zl, yy):
+        return own32[s, zl, yy] + crecv[s, zl, yy]
 
     def y_first(s):
-        ccopy[s].wait_recv()
-        two = own32[s, 2] + crecv[s, 2]
-        ytwo[s, 0] = two[:, :128].astype(bf16)
-        ytwo[s, 1] = two[:, 128:].astype(bf16)
+        for zl in range(2):
+            ccopy[s, zl].wait_recv()
+            ytwo[s, zl] = pair_sum(s, zl, y2).astype(bf16)
         yl2[s] = wires.start(ytwo.at[s, 0], yhl.at[s], up)
         yr2[s] = wires.start(ytwo.at[s, 1], yhr.at[s], down)
-        one = own32[s, 1] + crecv[s, 1]
-        own32[s, 1] = one
-        yright[s, 1] = one[:, 128:].astype(bf16)
+        yright[s, 1] = pair_sum(s, 1, y1).astype(bf16)
         yl[s, 1] = wires.start(yright.at[s, 1], yinl.at[s, 1], up)
-        one = own32[s, 3] + crecv[s, 3]
-        own32[s, 3] = one
-        yleft[s, 0] = one[:, :128].astype(bf16)
+        yleft[s, 0] = pair_sum(s, 0, y3).astype(bf16)
         yr[s, 0] = wires.start(yleft.at[s, 0], yinr.at[s, 0], down)
 
     def y_second(s):
         yl2[s].wait_recv()
-        yright[s, 0] = (own32[s, 1, :, :128] + yhl[s].astype(f32)).astype(bf16)
+        yright[s, 0] = (pair_sum(s, 0, y1) + yhl[s].astype(f32)).astype(bf16)
         yl[s, 0] = wires.start(yright.at[s, 0], yinl.at[s, 0], up)
         yr2[s].wait_recv()
-        yleft[s, 1] = (own32[s, 3, :, 128:] + yhr[s].astype(f32)).astype(bf16)
+        yleft[s, 1] = (pair_sum(s, 1, y3) + yhr[s].astype(f32)).astype(bf16)
         yr[s, 1] = wires.start(yleft.at[s, 1], yinr.at[s, 1], down)
 
     def place(s, zl):
         return pltpu.make_async_remote_copy(
-            src_ref=fsend.at[s, zl],
+            src_ref=xrecv.at[s, zl],
             dst_ref=frecv.at[z],
             send_sem=fsend_sems.at[s * 2 + zl],
             recv_sem=frecv_sems.at[z],
-            device_id=at(x_=(p + s) % NX, z_=2 * p + zl),
+            device_id=at(z_=(p + NX - s) % NX * 2 + zl),
             device_id_type=pl.DeviceIdType.MESH,
         )
+
+    move = {}
 
     def y_third(s):
         for zl in (1, 0):
             yl[s, zl].wait_recv()
             yr[s, zl].wait_recv()
-            lanes = slice(zl * 128, zl * 128 + 128)
-            out = own32[s, 0, :, lanes] + crecv[s, 0, :, lanes]
+            out = pair_sum(s, zl, y)
             out = out + yinl[s, zl].astype(f32) + yinr[s, zl].astype(f32)
-            fsend[s, zl] = out
             if s:
+                fsend[s, zl] = out.astype(bf16)
+                move[s, zl] = wires.start(fsend.at[s, zl], xrecv.at[s, zl], x_by(s))
+            else:
+                xrecv[s, zl] = out.astype(bf16)
+
+    def z_out(s):
+        for zl in (1, 0):
+            if s:
+                move[s, zl].wait_recv()
+            there_z = (p + NX - s) % NX * 2 + zl
+
+            @pl.when(z != there_z)
+            def _():
                 place(s, zl).start()
-            else:
-
-                @pl.when(z != 2 * p + zl)
-                def _():
-                    place(s, zl).start()
-
-                @pl.when(z == 2 * p + zl)
-                def _():
-                    frecv[z] = fsend[s, zl]
+
+            @pl.when(z == there_z)
+            def _():
+                frecv[z] = xrecv[s, zl]
 
     multiply(0)
     for t in (0, 1):
@@ -404,6 +441,7 @@
     multiply(1)
     y_first(3)
     y_third(0)
+    z_out(0)
     y_first(1)
     y_second(3)
     await_plane(rs1, rt_first)
@@ -422,13 +460,16 @@
     y_third(3)
     y_first(2)
     y_third(1)
+    z_out(3)
     y_second(2)
+    z_out(1)
     await_line(rs2, rt_first)
     total = rs2[0]
     for j in range(1, NZ):
         total = total + rs2[j]
     rt_col = columns_of(total)[:, 0:1]
     y_third(2)
+    z_out(2)
 
     own_cols = pl.ds(pl.multiple_of(v * 128, 128), 128)
     inv = inv_v[...]
@@ -436,53 +477,53 @@
     scale = inv * gain_ref[:, own_cols]
     for zs in range(NZ):
 
-        @pl.when(jnp.logical_or(foreign, zs != z))
+        @pl.when(zs != z)
         def _():
             pltpu.make_async_remote_copy(
                 src_ref=frecv.at[zs],
                 dst_ref=frecv.at[zs],
                 send_sem=fsend_sems.at[0],
                 recv_sem=frecv_sems.at[zs],
-                device_id=at(x_=source, z_=zs),
+                device_id=at(z_=zs),
                 device_id_type=pl.DeviceIdType.MESH,
             ).wait_recv()
 
-    total = frecv[0]
+    total = frecv[0].astype(f32)
     for zs in range(1, NZ):
-        total = total + frecv[zs]
-    grad_ref[...] = scale * total - minus
+        total = total + frecv[zs].astype(f32)
+    grad_ref[...] = scale * total.T - minus
 
     wires.close()
     for s in range(NX):
         for zl in range(2):
-            if s:
+
+            @pl.when(z != (p + NX - s) % NX * 2 + zl)
+            def _():
                 place(s, zl).wait_send()
-            else:
-
-                @pl.when(z != 2 * p + zl)
-                def _():
-                    place(s, zl).wait_send()
 
 
 def shards(hidden, head, gain, refusal_ids, refusal_count, loss_scale):
     V = pltpu.VMEM
     tile = (R, T)
     box = (R, 128)
-    wires = 120
+    wires = 140
     grad, log_refusal = pl.pallas_call(
         kernel,
         out_shape=(
             jax.ShapeDtypeStruct((R, 128), f32),
             jax.ShapeDtypeStruct((1, R), f32),
         ),
-        in_specs=[pl.BlockSpec(memory_space=pl.ANY)] * 2
-        + [pl.BlockSpec(memory_space=pltpu.VMEM)] * 4,
+        in_specs=[pl.BlockSpec(memory_space=pltpu.HBM)] * 6,
         out_specs=(pl.BlockSpec(memory_space=pltpu.VMEM),) * 2,
         scratch_shapes=[
             V((R, NX * DL), bf16),
             V((DL, VL), bf16),
+            V((1, NX * DL), f32),
+            V((16, R), jnp.int32),
+            V((1, R), jnp.int32),
+            V((1, R), f32),
             V(box, f32),
-            V((3, 4) + tile, bf16),
+            V((3,) + tile, bf16),
             V((NX, KT) + tile, bf16),
             V((VT,) + tile, f32),
             V((VT,) + tile, f32),
@@ -499,10 +540,10 @@
             V((NZ, 2, 8, 128), f32),
             V((NY * NC, 8, 128), f32),
             V((NZ, 8, 128), f32),
-            V((NX, VT) + tile, bf16),
-            V((NX, NY) + tile, f32),
-            V((NX, NY) + tile, f32),
-            V((NX, NY) + tile, f32),
+            V((NX, VT, T, R), bf16),
+            V((NX, 2, NY) + box, f32),
+            V((NX, 2, NY) + box, f32),
+            V((NX, 2, NY) + box, f32),
             V((NX, 2) + box, bf16),
             V((NX, 2) + box, bf16),
             V((NX, 2) + box, bf16),
@@ -510,23 +551,24 @@
             V((NX,) + box, bf16),
             V((NX, 2) + box, bf16),
             V((NX, 2) + box, bf16),
-            V((NX, 2) + box, f32),
-            V((NZ,) + box, f32),
-            pltpu.SemaphoreType.DMA((2,)),
+            V((NX, 2) + box, bf16),
+            V((NX, 2) + box, bf16),
+            V((NZ,) + box, bf16),
+            pltpu.SemaphoreType.DMA((6,)),
             pltpu.SemaphoreType.DMA((wires,)),
             pltpu.SemaphoreType.DMA((wires,)),
             pltpu.SemaphoreType.DMA((NX * 2,)),
             pltpu.SemaphoreType.DMA((NZ,)),
         ],
         compiler_params=pltpu.CompilerParams(
-            collective_id=0, has_side_effects=True, vmem_limit_bytes=48 << 20
+            collective_id=0, has_side_effects=True, vmem_limit_bytes=63 << 20
         ),
         name="head_grad",
     )(
         hidden,
         head,
         gain.reshape(1, -1),
-        refusal_ids,
+        refusal_ids.T,
         refusal_count.reshape(1, -1),
         loss_scale.reshape(1, -1),
     )

time: 112 us -> 92.5 us (0.83)
  Pallas kernels: 105 us -> 89.1 us
  local copies, waits for them, and re-layouts: 5.59 us -> 2.59 us
    pallas_call x1, Pallas kernels: 105 us -> 89.1 us  [shards(): pl.pallas_call(kernel, out_shape=(jax.ShapeDtypeStruct((R, 128), f32), ja...]
    unnamed x11 -> x2, local copies, waits for them, and re-layouts: 5.59 us -> 2.59 us
where the time goes in v2:
time: 92.5 us; the launch traced here: 92.4 us
  Pallas kernels  89.1 us (96%)
  local copies, waits for them, and re-layouts  2.59 us (3%)
    pallas_call x1, Pallas kernels, shards(): pl.pallas_call(kernel, out_shape=(jax.ShapeDtypeStruct((R, 128), f32), ja...  89.1 us
    unnamed x2, local copies, waits for them, and re-layouts  2.59 us

profile of v2, /device:TPU:4, one launch (start us, length us, event | category | flops | bytes accessed | tf_op | source)
XLA Modules:
  0.0 92.4 jit_solution(15960898204446262291)
XLA Ops:
  0.6 89.1 %head_grad.1 = (f32[128,128]{1,0:T(8,128)}, f32[1,128]{1,0:T(1,128)}) custom-call(bf16[128,8192]{1,0:T(8,128)(2,1)} %hid_hbm.1, bf16[2048,1024]{1,0:T(8,128)(2,1)} %head_hbm.1, f32[1,8192]{1,0:T(1,128)} %bitcast.5, s32[16,128]{1,0:T(8,128)} %bitcast.6, s32[1,128]{1,0:T(1,128)} %bitcast.7, f32[1,128]{1,0:T(1,128)} %bitcast.8), custom_call_target="tpu_custom_call" | custom-call | tf_op jit(solution)/shard_map/head_grad/pallas_call | solution.py:510
  89.8 1.5 %copy.10 = f32[128,128]{1,0:T(8,128)} copy(f32[128,128]{1,0:T(8,128)} %get-tuple-element.8) | data formatting | bytes 131072
  91.3 1.1 %copy.11 = f32[128]{0:T(128)} copy(f32[128]{0:T(128)} %bitcast.9) | data formatting | bytes 1024

commit v3 on v2

--- a/solution.py
+++ b/solution.py
@@ -49,8 +49,8 @@
 
 def kernel(
     hid_hbm, head_hbm, gain_hbm, ids_hbm, count_hbm, loss_hbm, grad_ref, log_ref,
-    hid, head, gain_ref, ids_ref, count_ref, loss_ref, inv_v, nsend, nrm, ptwo, pright, pleft, pown, hl, hr, inl, inr,
-    mask, eall, eref, st1, st2, rs1, rs2, gt, csend, crecv, own32,
+    hid, head, gain_ref, ids_ref, count_ref, loss_ref, inv_v, nfar, nsend, nrm, ptwo, pright, pleft, pown, hl, hr, inl, inr,
+    mask, eall, eref, st1, st2, rs1, rs2, gt, gs, lent, own32,
     ytwo, yright, yleft, yhl, yhr, yinl, yinr, fsend, xrecv, frecv,
     load_sems, send_sems, recv_sems, fsend_sems, frecv_sems,
 ):
@@ -130,74 +130,55 @@
         x = hid[:, pl.ds(col, T)].astype(f32)
         return (x * inv * gain_ref[:, pl.ds(col, T)]).astype(bf16)
 
-    k_own = c * NY + y
-    for d in (2, 1, 3):
-        nsend[d - 1] = normed((p + d) % NX * DL + k_own * T)
+    near = {d: c * NY + (y + d) % NY for d in range(NY)}
+    nfar[...] = normed((p + 2) % NX * DL + near[0] * T)
 
     pl.semaphore_wait(barrier, (NX - 1) + (NY * NC - 1) + (NZ - 1))
 
     up, down = y_by(1), y_by(NY - 1)
-    near = {d: c * NY + (y + d) % NY for d in range(NY)}
-    there = {d: (1 - c) * NY + (y + d) % NY for d in range(NY)}
-    first_half, second_half = pl.ds(0, R // 2), pl.ds(R // 2, R // 2)
-    come, go_up, go_down, far_up, far_down, shared = {}, {}, {}, {}, {}, {}
-    for d in (2, 1, 3):
-        slot = NX - d
-        come[slot] = wires.start(nsend.at[d - 1], nrm.at[slot, k_own], x_by(d))
+    right, left = x_by(1), x_by(NX - 1)
+    half, other_half = pl.ds(c * NY, NY), pl.ds((1 - c) * NY, NY)
+    come2 = wires.start(nfar, nrm.at[2, near[0]], x_by(2))
+    come, shared = {}, {}
+    for slot, i, device, d in ((3, 0, right, 1), (1, 1, left, NX - 1)):
+        for k in range(NY):
+            nsend[i, k] = normed((p + d) % NX * DL + (c * NY + k) * T)
+        come[slot] = wires.start(nsend.at[i], nrm.at[slot, half], device)
+
+    def piece(d):
+        return nrm.at[2, near[d]]
+
+    come2.wait_recv()
+    for d in (1, 3, 2):
+        wires.start(piece(0), piece(0), y_by(NY - d))
+    shared[0] = wires.start(piece(0), piece(0), sibling)
+    spread_at = dict(zip((1, 3, 2), range(wires.used - 4, wires.used - 1)))
     for k in range(KT):
         nrm[0, k] = normed(p * DL + k * T)
-
-    def share(slot, d):
-        shared[slot, d] = wires.used
-        wires.start(nrm.at[slot, near[d]], nrm.at[slot, near[d]], sibling)
-
-    def arrived(slot, d, device, index, rows=None):
-        piece = nrm.at[slot, near[d]] if rows is None else nrm.at[slot, near[d], rows]
-        wires.describe(piece, piece, device, index).wait_recv()
-
-    def near_out(slot):
+    for d in (1, 3, 2):
+        wires.describe(piece(d), piece(d), y_by(d), spread_at[d]).wait_recv()
+        shared[d] = wires.start(piece(d), piece(d), sibling)
+    shared_at = dict(zip((0, 1, 3, 2), (wires.used - 4, *range(wires.used - 3, wires.used))))
+
+    def share(slot):
         come[slot].wait_recv()
-        piece = nrm.at[slot, k_own]
-        go_up[slot] = wires.used
-        wires.start(piece, piece, up)
-        go_down[slot] = wires.used
-        wires.start(piece, piece, down)
-        share(slot, 0)
-
-    def far_out(slot):
-        arrived(slot, NY - 1, down, go_up[slot])
-        piece = nrm.at[slot, near[NY - 1], first_half]
-        far_up[slot] = wires.used
-        wires.start(piece, piece, up)
-        arrived(slot, 1, up, go_down[slot])
-        piece = nrm.at[slot, near[1], second_half]
-        far_down[slot] = wires.used
-        wires.start(piece, piece, down)
-        share(slot, NY - 1)
-        share(slot, 1)
-
-    def far_in(slot):
-        arrived(slot, 2, down, far_up[slot], first_half)
-        arrived(slot, 2, up, far_down[slot], second_half)
-        share(slot, 2)
+        rows = nrm.at[slot, half]
+        shared[slot, "at"] = wires.used
+        wires.start(rows, rows, sibling)
 
     def wait_share(slot):
-        for d in range(NY):
-            piece = nrm.at[slot, there[d]]
-            wires.describe(piece, piece, sibling, shared[slot, d]).wait_recv()
+        if slot == 2:
+            for d in range(NY):
+                rows = nrm.at[2, (1 - c) * NY + (y + d) % NY]
+                wires.describe(rows, rows, sibling, shared_at[d]).wait_recv()
+        else:
+            rows = nrm.at[slot, other_half]
+            wires.describe(rows, rows, sibling, shared[slot, "at"]).wait_recv()
 
     def partial(s, t):
         lhs = jnp.concatenate([nrm[s, k] for k in range(KT)], axis=1)
         return jnp.dot(lhs, head[:, t * T : (t + 1) * T], preferred_element_type=f32)
 
-    right, left = x_by(1), x_by(NX - 1)
-    near_out(2)
-    near_out(3)
-    near_out(1)
-    far_out(2)
-    far_in(2)
-    far_out(3)
-    far_out(1)
     load_head.wait()
     wait_share(2)
     ch_l, ch_r, cin_l, cin_r = {}, {}, {}, {}
@@ -207,8 +188,8 @@
             ch_l[t] = wires.start(ptwo.at[t], hl.at[t], right)
         else:
             ch_r[t - 2] = wires.start(ptwo.at[t], hr.at[t - 2], left)
-    far_in(3)
-    far_in(1)
+    share(3)
+    share(1)
     wait_share(1)
     for t in (2, 3):
         pright[t] = partial(1, t)
@@ -227,6 +208,10 @@
         ch_r[t].wait_recv()
         pleft[t + 2] = pleft[t + 2] + hr[t]
         cin_r[t + 2] = wires.start(pleft.at[t + 2], inr.at[t + 2], left)
+    lend = {}
+    for b in range(2 * NY):
+        rows = pl.ds(pl.multiple_of((b * NC + 1 - c) * 128, 128), 128)
+        lend[b] = wires.start(head.at[rows], lent.at[b], sibling)
     for t in range(VT):
         pown[t] = partial(0, t)
 
@@ -336,54 +321,58 @@
     for pair in ((0, 2), (1, 3)):
         for t in pair:
             g = eref[t] * f_ref - eall[t] * f_all
-            gt[0, t] = g.T.astype(bf16)
-            rt = rt + g.astype(bf16).astype(f32) * pown[t]
+            g = g.astype(bf16)
+            gt[0, t] = g
+            rt = rt + g.astype(f32) * pown[t]
         gather(*pair)
     gather(2, 0)
     gather(3, 1)
+    lot = {}
+
+    def to_sibling(s, t):
+        lot[s, t] = wires.start(gt.at[s, t], gs.at[s, t], sibling)
+
+    for t in (0, 2, 1, 3):
+        to_sibling(0, t)
     rt = jnp.sum(rt, axis=1, keepdims=True)
     rs1[j_own] = jnp.where(lane == 0, rt, jnp.zeros((R, 128), f32)).T[0:8]
     rt_first = spread_plane(rs1)
 
-    def grad_block(s, zl, cc):
-        rows = [
-            pl.multiple_of(((zl * NY + yy) * NC + cc) * 128, 128) for yy in range(NY)
-        ]
-        lhs = jnp.concatenate([head[pl.ds(row, 128), :] for row in rows], axis=0)
-        rhs = jnp.concatenate([gt[s, t] for t in range(VT)], axis=0)
-        out = jnp.dot(lhs, rhs, preferred_element_type=f32)
-        return out.reshape(NY, 128, R)
-
-    ccopy, yl2, yr2, yl, yr = {}, {}, {}, {}, {}
+    yl2, yr2, yl, yr = {}, {}, {}, {}
     y1, y2, y3 = ((y + d) % NY for d in (1, 2, 3))
 
     def multiply(s):
+        for t in range(VT):
+            lot[s, t].wait_recv()
+        mine = jnp.concatenate([gt[s, t] for t in range(VT)], axis=1)
+        other = jnp.concatenate([gs[s, t] for t in range(VT)], axis=1)
         for zl in range(2):
-            csend[s, zl] = grad_block(s, zl, 1 - c)
-            ccopy[s, zl] = wires.start(csend.at[s, zl], crecv.at[s, zl], sibling)
-        for zl in range(2):
-            own32[s, zl] = grad_block(s, zl, c)
-
-    def pair_sum(s, zl, yy):
-        return own32[s, zl, yy] + crecv[s, zl, yy]
+            rows = [
+                pl.multiple_of(((zl * NY + yy) * NC + c) * 128, 128)
+                for yy in range(NY)
+            ]
+            here = jnp.concatenate([head[pl.ds(row, 128), :] for row in rows], axis=0)
+            from_lent = lent[zl * NY : (zl + 1) * NY].reshape(NY * 128, VL)
+            out = jnp.dot(here, mine.T, preferred_element_type=f32)
+            out = out + jnp.dot(from_lent, other.T, preferred_element_type=f32)
+            own32[s, zl] = out.reshape(NY, 128, R)
 
     def y_first(s):
         for zl in range(2):
-            ccopy[s, zl].wait_recv()
-            ytwo[s, zl] = pair_sum(s, zl, y2).astype(bf16)
+            ytwo[s, zl] = own32[s, zl, y2].astype(bf16)
         yl2[s] = wires.start(ytwo.at[s, 0], yhl.at[s], up)
         yr2[s] = wires.start(ytwo.at[s, 1], yhr.at[s], down)
-        yright[s, 1] = pair_sum(s, 1, y1).astype(bf16)
+        yright[s, 1] = own32[s, 1, y1].astype(bf16)
         yl[s, 1] = wires.start(yright.at[s, 1], yinl.at[s, 1], up)
-        yleft[s, 0] = pair_sum(s, 0, y3).astype(bf16)
+        yleft[s, 0] = own32[s, 0, y3].astype(bf16)
         yr[s, 0] = wires.start(yleft.at[s, 0], yinr.at[s, 0], down)
 
     def y_second(s):
         yl2[s].wait_recv()
-        yright[s, 0] = (pair_sum(s, 0, y1) + yhl[s].astype(f32)).astype(bf16)
+        yright[s, 0] = (own32[s, 0, y1] + yhl[s].astype(f32)).astype(bf16)
         yl[s, 0] = wires.start(yright.at[s, 0], yinl.at[s, 0], up)
         yr2[s].wait_recv()
-        yleft[s, 1] = (pair_sum(s, 1, y3) + yhr[s].astype(f32)).astype(bf16)
+        yleft[s, 1] = (own32[s, 1, y3] + yhr[s].astype(f32)).astype(bf16)
         yr[s, 1] = wires.start(yleft.at[s, 1], yinr.at[s, 1], down)
 
     def place(s, zl):
@@ -402,7 +391,7 @@
         for zl in (1, 0):
             yl[s, zl].wait_recv()
             yr[s, zl].wait_recv()
-            out = pair_sum(s, zl, y)
+            out = own32[s, zl, y]
             out = out + yinl[s, zl].astype(f32) + yinr[s, zl].astype(f32)
             if s:
                 fsend[s, zl] = out.astype(bf16)
@@ -424,51 +413,57 @@
             def _():
                 frecv[z] = xrecv[s, zl]
 
+    for b in range(2 * NY):
+        lend[b].wait_recv()
     multiply(0)
     for t in (0, 1):
         to_right[t].wait_recv()
         wires.start(gt.at[3, t], gt.at[2, t], right)
         to_left[t + 2].wait_recv()
         wires.start(gt.at[1, t + 2], gt.at[2, t + 2], left)
-    forward = wires.used - 4
+        to_sibling(3, t)
+        to_sibling(1, t + 2)
+    forward = wires.used - 8
     y_first(0)
     for t in (2, 3):
         to_right[t].wait_recv()
+        to_sibling(3, t)
+        to_left[t - 2].wait_recv()
+        to_sibling(1, t - 2)
+    y_second(0)
     multiply(3)
-    y_second(0)
-    for t in (0, 1):
-        to_left[t].wait_recv()
+    y_first(3)
     multiply(1)
-    y_first(3)
+    y_first(1)
     y_third(0)
     z_out(0)
-    y_first(1)
-    y_second(3)
+    for t in (0, 1):
+        for i, tile, device in ((0, t, left), (1, t + 2, right)):
+            wires.describe(
+                gt.at[2, tile], gt.at[2, tile], device, forward + 4 * t + i
+            ).wait_recv()
+            to_sibling(2, tile)
+    multiply(2)
+    y_first(2)
     await_plane(rs1, rt_first)
     total = rs1[0]
     for j in range(1, NY * NC):
         total = total + rs1[j]
     rs2[z] = total
     rt_first = spread_line(rs2)
-    for t in (0, 1):
-        for i, tile, device in ((0, t, left), (1, t + 2, right)):
-            wires.describe(
-                gt.at[2, tile], gt.at[2, tile], device, forward + 2 * t + i
-            ).wait_recv()
-    multiply(2)
+    y_second(3)
     y_second(1)
+    y_second(2)
     y_third(3)
-    y_first(2)
     y_third(1)
+    y_third(2)
     z_out(3)
-    y_second(2)
     z_out(1)
     await_line(rs2, rt_first)
     total = rs2[0]
     for j in range(1, NZ):
         total = total + rs2[j]
     rt_col = columns_of(total)[:, 0:1]
-    y_third(2)
     z_out(2)
 
     own_cols = pl.ds(pl.multiple_of(v * 128, 128), 128)
@@ -523,7 +518,8 @@
             V((1, R), jnp.int32),
             V((1, R), f32),
             V(box, f32),
-            V((3,) + tile, bf16),
+            V(tile, bf16),
+            V((2, NY) + tile, bf16),
             V((NX, KT) + tile, bf16),
             V((VT,) + tile, f32),
             V((VT,) + tile, f32),
@@ -540,9 +536,9 @@
             V((NZ, 2, 8, 128), f32),
             V((NY * NC, 8, 128), f32),
             V((NZ, 8, 128), f32),
-            V((NX, VT, T, R), bf16),
-            V((NX, 2, NY) + box, f32),
-            V((NX, 2, NY) + box, f32),
+            V((NX, VT) + tile, bf16),
+            V((NX, VT) + tile, bf16),
+            V((2 * NY, 128, VL), bf16),
             V((NX, 2, NY) + box, f32),
             V((NX, 2) + box, bf16),
             V((NX, 2) + box, bf16),

time: 92.5 us -> 87.3 us (0.944)
  Pallas kernels: 89.1 us -> 83.2 us
    pallas_call x1, Pallas kernels: 89.1 us -> 83.2 us  [shards(): pl.pallas_call(kernel, out_shape=(jax.ShapeDtypeStruct((R, 128), f32), ja...]
where the time goes in v3:
time: 87.3 us; the launch traced here: 86.4 us
  Pallas kernels  83.2 us (95%)
  local copies, waits for them, and re-layouts  2.59 us (3%)
    pallas_call x1, Pallas kernels, shards(): pl.pallas_call(kernel, out_shape=(jax.ShapeDtypeStruct((R, 128), f32), ja...  83.2 us
    unnamed x2, local copies, waits for them, and re-layouts  2.59 us

profile of v3, /device:TPU:4, one launch (start us, length us, event | category | flops | bytes accessed | tf_op | source)
XLA Modules:
  0.0 86.4 jit_solution(10401863452087407042)
XLA Ops:
  0.6 83.2 %head_grad.1 = (f32[128,128]{1,0:T(8,128)}, f32[1,128]{1,0:T(1,128)}) custom-call(bf16[128,8192]{1,0:T(8,128)(2,1)} %hid_hbm.1, bf16[2048,1024]{1,0:T(8,128)(2,1)} %head_hbm.1, f32[1,8192]{1,0:T(1,128)} %bitcast.5, s32[16,128]{1,0:T(8,128)} %bitcast.6, s32[1,128]{1,0:T(1,128)} %bitcast.7, f32[1,128]{1,0:T(1,128)} %bitcast.8), custom_call_target="tpu_custom_call" | custom-call | tf_op jit(solution)/shard_map/head_grad/pallas_call | solution.py:505
  83.8 1.5 %copy.10 = f32[128,128]{1,0:T(8,128)} copy(f32[128,128]{1,0:T(8,128)} %get-tuple-element.8) | data formatting | bytes 131072
  85.3 1.1 %copy.11 = f32[128]{0:T(128)} copy(f32[128]{0:T(128)} %bitcast.9) | data formatting | bytes 1024

commit v4 on v3

--- a/solution.py
+++ b/solution.py
@@ -103,6 +103,14 @@
         greet(plane_by(d)[0])
     for d in range(1, NZ):
         greet(z_by(d))
+    corners = [(1, 1), (1, NZ - 1), (NY - 1, 1), (NY - 1, NZ - 1)]
+
+    def corner(i):
+        return at(y_=(y + corners[i][0]) % NY, z_=(z + corners[i][1]) % NZ)
+
+    for i in range(4):
+        greet(corner(i))
+
     wires = Wires(send_sems, recv_sems)
 
     lane = lax.broadcasted_iota(jnp.int32, (R, 128), 1)
@@ -130,35 +138,55 @@
         x = hid[:, pl.ds(col, T)].astype(f32)
         return (x * inv * gain_ref[:, pl.ds(col, T)]).astype(bf16)
 
-    near = {d: c * NY + (y + d) % NY for d in range(NY)}
-    nfar[...] = normed((p + 2) % NX * DL + near[0] * T)
-
-    pl.semaphore_wait(barrier, (NX - 1) + (NY * NC - 1) + (NZ - 1))
+    def piece_of(cc, dy, dz):
+        return cc * 4 + (y + dy) % 2 * 2 + (z + dz) % 2
+
+    nfar[...] = normed((p + 2) % NX * DL + piece_of(c, 0, 0) * T)
+
+    pl.semaphore_wait(barrier, (NX - 1) + (NY * NC - 1) + (NZ - 1) + 4)
 
     up, down = y_by(1), y_by(NY - 1)
     right, left = x_by(1), x_by(NX - 1)
     half, other_half = pl.ds(c * NY, NY), pl.ds((1 - c) * NY, NY)
-    come2 = wires.start(nfar, nrm.at[2, near[0]], x_by(2))
+    own_piece = piece_of(c, 0, 0)
+    come2 = wires.start(nfar, nrm.at[2, own_piece], x_by(2))
     come, shared = {}, {}
     for slot, i, device, d in ((3, 0, right, 1), (1, 1, left, NX - 1)):
         for k in range(NY):
             nsend[i, k] = normed((p + d) % NX * DL + (c * NY + k) * T)
         come[slot] = wires.start(nsend.at[i], nrm.at[slot, half], device)
 
-    def piece(d):
-        return nrm.at[2, near[d]]
-
+    def rows_of(piece, i, n):
+        return nrm.at[2, piece, pl.ds(i * (R // n), R // n)]
+
+    sides = (up, down, z_by(1), z_by(NZ - 1))
     come2.wait_recv()
-    for d in (1, 3, 2):
-        wires.start(piece(0), piece(0), y_by(NY - d))
-    shared[0] = wires.start(piece(0), piece(0), sibling)
-    spread_at = dict(zip((1, 3, 2), range(wires.used - 4, wires.used - 1)))
+    spread_at = wires.used
+    for i in range(4):
+        part = rows_of(own_piece, i, 4)
+        wires.start(part, part, corner(i))
+    for i in range(4):
+        part = rows_of(own_piece, i % 2, 2)
+        wires.start(part, part, sides[i])
+
+    def share_piece(dy, dz):
+        whole = nrm.at[2, piece_of(c, dy, dz)]
+        shared_at[dy, dz] = wires.used
+        wires.start(whole, whole, sibling)
+
+    shared_at = {}
+    share_piece(0, 0)
     for k in range(KT):
         nrm[0, k] = normed(p * DL + k * T)
-    for d in (1, 3, 2):
-        wires.describe(piece(d), piece(d), y_by(d), spread_at[d]).wait_recv()
-        shared[d] = wires.start(piece(d), piece(d), sibling)
-    shared_at = dict(zip((0, 1, 3, 2), (wires.used - 4, *range(wires.used - 3, wires.used))))
+    for dy, dz, first in ((1, 0, 0), (0, 1, 2)):
+        for i in range(2):
+            part = rows_of(piece_of(c, dy, dz), i, 2)
+            wires.describe(part, part, sides[first + i], spread_at + 4 + first + i).wait_recv()
+        share_piece(dy, dz)
+    for i in range(4):
+        part = rows_of(piece_of(c, 1, 1), i, 4)
+        wires.describe(part, part, corner(i), spread_at + i).wait_recv()
+    share_piece(1, 1)
 
     def share(slot):
         come[slot].wait_recv()
@@ -168,9 +196,9 @@
 
     def wait_share(slot):
         if slot == 2:
-            for d in range(NY):
-                rows = nrm.at[2, (1 - c) * NY + (y + d) % NY]
-                wires.describe(rows, rows, sibling, shared_at[d]).wait_recv()
+            for (dy, dz), index in shared_at.items():
+                rows = nrm.at[2, piece_of(1 - c, dy, dz)]
+                wires.describe(rows, rows, sibling, index).wait_recv()
         else:
             rows = nrm.at[slot, other_half]
             wires.describe(rows, rows, sibling, shared[slot, "at"]).wait_recv()
@@ -342,30 +370,34 @@
     y1, y2, y3 = ((y + d) % NY for d in (1, 2, 3))
 
     def multiply(s):
-        for t in range(VT):
-            lot[s, t].wait_recv()
-        mine = jnp.concatenate([gt[s, t] for t in range(VT)], axis=1)
-        other = jnp.concatenate([gs[s, t] for t in range(VT)], axis=1)
+        def times(block, tiles):
+            rhs = jnp.concatenate([tiles[s, t] for t in range(VT)], axis=1).T
+            return jnp.dot(block, rhs, preferred_element_type=f32).reshape(NY, 128, R)
+
         for zl in range(2):
             rows = [
                 pl.multiple_of(((zl * NY + yy) * NC + c) * 128, 128)
                 for yy in range(NY)
             ]
             here = jnp.concatenate([head[pl.ds(row, 128), :] for row in rows], axis=0)
-            from_lent = lent[zl * NY : (zl + 1) * NY].reshape(NY * 128, VL)
-            out = jnp.dot(here, mine.T, preferred_element_type=f32)
-            out = out + jnp.dot(from_lent, other.T, preferred_element_type=f32)
-            own32[s, zl] = out.reshape(NY, 128, R)
-
-    def y_first(s):
+            own32[s, zl] = times(here, gt)
+        for t in range(VT):
+            lot[s, t].wait_recv()
         for zl in range(2):
-            ytwo[s, zl] = own32[s, zl, y2].astype(bf16)
-        yl2[s] = wires.start(ytwo.at[s, 0], yhl.at[s], up)
-        yr2[s] = wires.start(ytwo.at[s, 1], yhr.at[s], down)
-        yright[s, 1] = own32[s, 1, y1].astype(bf16)
-        yl[s, 1] = wires.start(yright.at[s, 1], yinl.at[s, 1], up)
-        yleft[s, 0] = own32[s, 0, y3].astype(bf16)
-        yr[s, 0] = wires.start(yleft.at[s, 0], yinr.at[s, 0], down)
+            block = lent[zl * NY : (zl + 1) * NY].reshape(NY * 128, VL)
+            own32[s, zl] = own32[s, zl] + times(block, gs)
+            y_first(s, zl)
+
+    def y_first(s, zl):
+        ytwo[s, zl] = own32[s, zl, y2].astype(bf16)
+        if zl == 0:
+            yl2[s] = wires.start(ytwo.at[s, 0], yhl.at[s], up)
+            yleft[s, 0] = own32[s, 0, y3].astype(bf16)
+            yr[s, 0] = wires.start(yleft.at[s, 0], yinr.at[s, 0], down)
+        else:
+            yr2[s] = wires.start(ytwo.at[s, 1], yhr.at[s], down)
+            yright[s, 1] = own32[s, 1, y1].astype(bf16)
+            yl[s, 1] = wires.start(yright.at[s, 1], yinl.at[s, 1], up)
 
     def y_second(s):
         yl2[s].wait_recv()
@@ -424,7 +456,6 @@
         to_sibling(3, t)
         to_sibling(1, t + 2)
     forward = wires.used - 8
-    y_first(0)
     for t in (2, 3):
         to_right[t].wait_recv()
         to_sibling(3, t)
@@ -432,9 +463,7 @@
         to_sibling(1, t - 2)
     y_second(0)
     multiply(3)
-    y_first(3)
     multiply(1)
-    y_first(1)
     y_third(0)
     z_out(0)
     for t in (0, 1):
@@ -444,7 +473,6 @@
             ).wait_recv()
             to_sibling(2, tile)
     multiply(2)
-    y_first(2)
     await_plane(rs1, rt_first)
     total = rs1[0]
     for j in range(1, NY * NC):

time: 87.3 us -> 85.8 us (0.983)
  no operation moved by 1% of the time
where the time goes in v4:
time: 85.8 us; the launch traced here: 85.7 us
  Pallas kernels  82.4 us (96%)
  local copies, waits for them, and re-layouts  2.59 us (3%)
    pallas_call x1, Pallas kernels, shards(): pl.pallas_call(kernel, out_shape=(jax.ShapeDtypeStruct((R, 128), f32), ja...  82.4 us
    unnamed x2, local copies, waits for them, and re-layouts  2.59 us

profile of v4, /device:TPU:4, one launch (start us, length us, event | category | flops | bytes accessed | tf_op | source)
XLA Modules:
  0.0 85.7 jit_solution(4518754092432506425)
XLA Ops:
  0.6 82.4 %head_grad.1 = (f32[128,128]{1,0:T(8,128)}, f32[1,128]{1,0:T(1,128)}) custom-call(bf16[128,8192]{1,0:T(8,128)(2,1)} %hid_hbm.1, bf16[2048,1024]{1,0:T(8,128)(2,1)} %head_hbm.1, f32[1,8192]{1,0:T(1,128)} %bitcast.5, s32[16,128]{1,0:T(8,128)} %bitcast.6, s32[1,128]{1,0:T(1,128)} %bitcast.7, f32[1,128]{1,0:T(1,128)} %bitcast.8), custom_call_target="tpu_custom_call" | custom-call | tf_op jit(solution)/shard_map/head_grad/pallas_call | solution.py:533
  83.1 1.5 %copy.10 = f32[128,128]{1,0:T(8,128)} copy(f32[128,128]{1,0:T(8,128)} %get-tuple-element.8) | data formatting | bytes 131072
  84.5 1.1 %copy.11 = f32[128]{0:T(128)} copy(f32[128]{0:T(128)} %bitcast.9) | data formatting | bytes 1024

commit v5 on v4

--- a/solution.py
+++ b/solution.py
@@ -151,10 +151,9 @@
     own_piece = piece_of(c, 0, 0)
     come2 = wires.start(nfar, nrm.at[2, own_piece], x_by(2))
     come, shared = {}, {}
-    for slot, i, device, d in ((3, 0, right, 1), (1, 1, left, NX - 1)):
+    for i, d in ((0, 1), (1, NX - 1)):
         for k in range(NY):
             nsend[i, k] = normed((p + d) % NX * DL + (c * NY + k) * T)
-        come[slot] = wires.start(nsend.at[i], nrm.at[slot, half], device)
 
     def rows_of(piece, i, n):
         return nrm.at[2, piece, pl.ds(i * (R // n), R // n)]
@@ -168,6 +167,9 @@
     for i in range(4):
         part = rows_of(own_piece, i % 2, 2)
         wires.start(part, part, sides[i])
+
+    come[3] = wires.start(nsend.at[0], nrm.at[3, half], right)
+    come[1] = wires.start(nsend.at[1], nrm.at[1, half], left)
 
     def share_piece(dy, dz):
         whole = nrm.at[2, piece_of(c, dy, dz)]
@@ -294,27 +296,29 @@
     st1[j_own, 0] = packed[0:8]
     st1[j_own, 1] = packed[8:16]
 
+    far_first = (4, 3, 5, 2, 6, 1, 7)
+
     def spread_plane(buf):
         first = wires.used
-        for d in range(1, NY * NC):
+        for d in far_first:
             wires.start(buf.at[j_own], buf.at[j_own], plane_by(d)[0])
         return first
 
     def await_plane(buf, first):
-        for d in range(1, NY * NC):
+        for i, d in enumerate(far_first):
             device, j = plane_by(NY * NC - d)
-            wires.describe(buf.at[j], buf.at[j], device, first + d - 1).wait_recv()
+            wires.describe(buf.at[j], buf.at[j], device, first + i).wait_recv()
 
     def spread_line(buf):
         first = wires.used
-        for d in range(1, NZ):
+        for d in far_first:
             wires.start(buf.at[z], buf.at[z], z_by(d))
         return first
 
     def await_line(buf, first):
-        for d in range(1, NZ):
+        for i, d in enumerate(far_first):
             zz = (z + NZ - d) % NZ
-            wires.describe(buf.at[zz], buf.at[zz], at(z_=zz), first + d - 1).wait_recv()
+            wires.describe(buf.at[zz], buf.at[zz], at(z_=zz), first + i).wait_recv()
 
     def merged(buf, n):
         peak = buf[0, 0]
@@ -466,6 +470,12 @@
     multiply(1)
     y_third(0)
     z_out(0)
+    await_plane(rs1, rt_first)
+    total = rs1[0]
+    for j in range(1, NY * NC):
+        total = total + rs1[j]
+    rs2[z] = total
+    rt_first = spread_line(rs2)
     for t in (0, 1):
         for i, tile, device in ((0, t, left), (1, t + 2, right)):
             wires.describe(
@@ -473,12 +483,6 @@
             ).wait_recv()
             to_sibling(2, tile)
     multiply(2)
-    await_plane(rs1, rt_first)
-    total = rs1[0]
-    for j in range(1, NY * NC):
-        total = total + rs1[j]
-    rs2[z] = total
-    rt_first = spread_line(rs2)
     y_second(3)
     y_second(1)
     y_second(2)

time: 85.8 us -> 84.9 us (0.990)
  Pallas kernels: 82.4 us -> 81.5 us
    pallas_call x1, Pallas kernels: 82.4 us -> 81.5 us  [shards(): pl.pallas_call(kernel, out_shape=(jax.ShapeDtypeStruct((R, 128), f32), ja...]
where the time goes in v5:
time: 84.9 us; the launch traced here: 84.8 us
  Pallas kernels  81.5 us (96%)
  local copies, waits for them, and re-layouts  2.59 us (3%)
    pallas_call x1, Pallas kernels, shards(): pl.pallas_call(kernel, out_shape=(jax.ShapeDtypeStruct((R, 128), f32), ja...  81.5 us
    unnamed x2, local copies, waits for them, and re-layouts  2.59 us

profile of v5, /device:TPU:4, one launch (start us, length us, event | category | flops | bytes accessed | tf_op | source)
XLA Modules:
  0.0 84.8 jit_solution(6049637415196877057)
XLA Ops:
  0.6 81.5 %head_grad.1 = (f32[128,128]{1,0:T(8,128)}, f32[1,128]{1,0:T(1,128)}) custom-call(bf16[128,8192]{1,0:T(8,128)(2,1)} %hid_hbm.1, bf16[2048,1024]{1,0:T(8,128)(2,1)} %head_hbm.1, f32[1,8192]{1,0:T(1,128)} %bitcast.5, s32[16,128]{1,0:T(8,128)} %bitcast.6, s32[1,128]{1,0:T(1,128)} %bitcast.7, f32[1,128]{1,0:T(1,128)} %bitcast.8), custom_call_target="tpu_custom_call" | custom-call | tf_op jit(solution)/shard_map/head_grad/pallas_call | solution.py:537
  82.2 1.5 %copy.10 = f32[128,128]{1,0:T(8,128)} copy(f32[128,128]{1,0:T(8,128)} %get-tuple-element.8) | data formatting | bytes 131072
  83.6 1.1 %copy.11 = f32[128]{0:T(128)} copy(f32[128]{0:T(128)} %bitcast.9) | data formatting | bytes 1024

commit v6 on v5

--- a/solution.py
+++ b/solution.py
@@ -486,9 +486,9 @@
     y_second(3)
     y_second(1)
     y_second(2)
+    y_third(2)
     y_third(3)
     y_third(1)
-    y_third(2)
     z_out(3)
     z_out(1)
     await_line(rs2, rt_first)

time: 84.9 us -> 86.4 us (1.018); the launches traced: 84.8 us -> 85.2 us
  no operation moved by 1% of the time
where the time goes in v6:
time: 86.4 us; the launch traced here: 85.2 us
  Pallas kernels  82 us (95%)
  local copies, waits for them, and re-layouts  2.59 us (3%)
    pallas_call x1, Pallas kernels, shards(): pl.pallas_call(kernel, out_shape=(jax.ShapeDtypeStruct((R, 128), f32), ja...  82 us
    unnamed x2, local copies, waits for them, and re-layouts  2.59 us

profile of v6, /device:TPU:4, one launch (start us, length us, event | category | flops | bytes accessed | tf_op | source)
XLA Modules:
  0.0 85.2 jit_solution(16449821838903470830)
XLA Ops:
  0.6 82.0 %head_grad.1 = (f32[128,128]{1,0:T(8,128)}, f32[1,128]{1,0:T(1,128)}) custom-call(bf16[128,8192]{1,0:T(8,128)(2,1)} %hid_hbm.1, bf16[2048,1024]{1,0:T(8,128)(2,1)} %head_hbm.1, f32[1,8192]{1,0:T(1,128)} %bitcast.5, s32[16,128]{1,0:T(8,128)} %bitcast.6, s32[1,128]{1,0:T(1,128)} %bitcast.7, f32[1,128]{1,0:T(1,128)} %bitcast.8), custom_call_target="tpu_custom_call" | custom-call | tf_op jit(solution)/shard_map/head_grad/pallas_call | solution.py:537
  82.7 1.5 %copy.10 = f32[128,128]{1,0:T(8,128)} copy(f32[128,128]{1,0:T(8,128)} %get-tuple-element.8) | data formatting | bytes 131072
  84.1 1.1 %copy.11 = f32[128]{0:T(128)} copy(f32[128]{0:T(128)} %bitcast.9) | data formatting | bytes 1024
